TPU v7x, 256 devices: a whole 4x4x8 slice. The times are simulated.
256 devices in a mesh: ka: 8 (over y_lo, x), pw: 32 (over y_hi, z, core).
Axes of the slice: x: 4, y: 4 (y_hi: 2, y_lo: 2; y = y_hi * 2 + y_lo), z: 8, core: 2. Of those that a mesh axis runs over, the one named last changes fastest.
Arguments:
- states_re: bfloat16 [16, 512, 32768], P('ka', None, 'pw'), may hold values from -0.016572815 to 0.016572815
- states_im: bfloat16 [16, 512, 32768], P('ka', None, 'pw'), may hold values from -0.016572815 to 0.016572815
Outputs:
- wilson_lines: float32 [16, 512, 2, 512], P('ka', 'pw')
All inputs are finite; a program needn't handle non-finite values.
Results may differ from a plain program's by a relative error of at most 0.0003.
Values may be sent and summed in bfloat16 or wider, within the bound.
A program may use at most 64 MiB of HBM per device.

v0:
```python
import jax
import jax.numpy as jnp
from jax import lax
from jax.sharding import PartitionSpec as P


def from_behind(block, axis, distance):
    devices = range(lax.axis_size(axis))
    route = [((i - distance) % len(devices), i) for i in devices]
    return lax.ppermute(block, axis, route)


def shifted(shard, axis, by):
    size = lax.axis_size(axis)
    pairs = [(i, i + by) for i in range(size) if 0 <= i + by < size]
    return lax.ppermute(shard, axis, pairs)


def complex_rows(left, right):
    highest = lax.Precision.HIGHEST
    left_re = left[:, 0]
    left_im = left[:, 1]
    right_re = right[:, 0]
    right_im = right[:, 1]
    real_part = jnp.dot(
        left_re, right_re, precision=highest, preferred_element_type=jnp.float32
    ) - jnp.dot(left_im, right_im, precision=highest, preferred_element_type=jnp.float32)
    imag_part = jnp.dot(
        left_re, right_im, precision=highest, preferred_element_type=jnp.float32
    ) + jnp.dot(left_im, right_re, precision=highest, preferred_element_type=jnp.float32)
    return jnp.stack([real_part, imag_part], 1)


def shards(states_re, states_im):
    kcount = states_re.shape[0]
    bands = states_re.shape[1]
    pw_width = lax.axis_size("pw")
    ka_width = lax.axis_size("ka")
    band_rows = bands // pw_width
    ka_place = lax.axis_index("ka")
    first_band = lax.axis_index("pw") * band_rows
    next_re, next_im = from_behind((states_re[:1], states_im[:1]), "ka", -1)
    after_re = jnp.concatenate([states_re[1:], next_re], 0)
    after_im = jnp.concatenate([states_im[1:], next_im], 0)
    real_part = jnp.einsum(
        "kbg,kcg->bkc", states_re, after_re, preferred_element_type=jnp.float32
    ) + jnp.einsum("kbg,kcg->bkc", states_im, after_im, preferred_element_type=jnp.float32)
    imag_part = jnp.einsum(
        "kbg,kcg->bkc", states_re, after_im, preferred_element_type=jnp.float32
    ) - jnp.einsum("kbg,kcg->bkc", states_im, after_re, preferred_element_type=jnp.float32)
    margin_rows = lax.psum_scatter(
        jnp.stack([real_part, imag_part], 2), "pw", scatter_dimension=0, tiled=True
    )
    margin_full = lax.all_gather(margin_rows, "pw", axis=0, tiled=True)
    row_index = lax.broadcasted_iota(jnp.int32, (band_rows, bands), 0) + first_band
    col_index = lax.broadcasted_iota(jnp.int32, (band_rows, bands), 1)
    eye_real = (row_index == col_index).astype(jnp.float32)
    eye_rows = jnp.stack([eye_real, jnp.zeros_like(eye_real)], 1)

    def sweep(start_rows):
        current = start_rows
        collected = []
        for kpoint in range(kcount):
            current = complex_rows(current, margin_full[:, kpoint])
            collected.append(current)
        return jnp.stack(collected, 0)

    own_span = sweep(eye_rows)[-1]
    span_whole = lax.all_gather(own_span, "pw", axis=0, tiled=True)

    def advance(position, start_rows):
        last_line = complex_rows(start_rows, span_whole)
        received = shifted(last_line, "ka", 1)
        return jnp.where(ka_place == position + 1, received, start_rows)

    start_rows = lax.fori_loop(0, ka_width - 1, advance, eye_rows)
    return sweep(start_rows)


def solution(mesh):
    in_specs = (P("ka", None, "pw"), P("ka", None, "pw"))
    out_specs = P("ka", "pw", None, None)
    return jax.shard_map(shards, mesh=mesh, in_specs=in_specs, out_specs=out_specs, check_vma=False)
```

profile of v0, /device:TPU:8, one launch (start us, length us, event | category | flops | bytes accessed | tf_op | source)
XLA Modules:
  0.0 635.8 jit_solution(6827714051969218923)
XLA Ops:
  6.5 1.9 fusion.87
  8.4 2.7 collective-permute-start.2
  12.2 22.5 %collective-permute-done.2 = bf16[1,512,1024]{2,1,0:T(8,128)(2,1)S(1)} collective-permute-done((bf16[1,512,1024]{2,1,0:T(8,128)(2,1)S(1)}, bf16[1,512,1024]{2,1,0:T(8,128)(2,1)S(1)}, u32[]{:S(2)}, u32[]{:S(2)}) %collective-permute-start.2) | collective-permute-done | bytes 1048608 | tf_op jit(solution)/shard_map/ppermute | solution.py:10
  36.0 20.1 %collective-permute-done.1 = bf16[1,512,1024]{2,1,0:T(8,128)(2,1)S(1)} collective-permute-done((bf16[1,512,1024]{2,1,0:T(8,128)(2,1)S(1)}, bf16[1,512,1024]{2,1,0:T(8,128)(2,1)S(1)}, u32[]{:S(2)}, u32[]{:S(2)}) %collective-permute-start.1) | collective-permute-done | bytes 1048608 | tf_op jit(solution)/shard_map/ppermute | solution.py:10
  59.9 2.4 pad_maximum_fusion.1
  62.3 7.3 %copy.5 = f32[512,2,2,512]{3,2,1,0:T(2,128)} copy(f32[512,2,2,512]{0,3,1,2:T(8,128)} %pad_maximum_fusion.1) | data formatting | bytes 8388608 | tf_op jit(solution)/shard_map/stack | solution.py:52
  71.6 281.8 %all-reduce.4.cloned.1.call-done = f32[512,2,2,512]{3,2,1,0:T(2,128)} async-done(((f32[512,2,2,512]{3,2,1,0:T(2,128)}), f32[512,2,2,512]{3,2,1,0:T(2,128)}) %all-reduce.4.cloned.1.call-update) | async-done | bytes 4194320
  355.0 86.2 %all-gather.3.cloned.1.call-done = f32[512,2,2,512]{3,2,1,0:T(2,128)} async-done(((f32[16,2,2,512]{3,2,1,0:T(2,128)}), f32[512,2,2,512]{3,2,1,0:T(2,128)}) %all-gather.3.cloned.1.call-update) | async-done | bytes 4194320 | tf_op jit(solution)/shard_map/all_gather | solution.py:54
  441.2 3.7 slice_bitcast_fusion
  444.9 3.5 fusion.85
  453.8 76.6 %all-gather.5.cloned.1.call-done = f32[512,2,512]{2,0,1:T(8,128)} async-done(((f32[16,2,512]{2,0,1:T(8,128)}), f32[512,2,512]{2,0,1:T(8,128)}) %all-gather.5.cloned.1.call-update) | async-done | bytes 2097168 | tf_op jit(solution)/shard_map/all_gather | solution.py:69
  530.4 3.2 copy.6
  533.6 87.2 %while.13 = (s32[]{:T(128)}, f32[16,2,512]{2,0,1:T(8,128)S(1)}, s32[]{:T(128)}, f32[512,2,512]{2,1,0:T(2,128)S(1)}, s32[]{:T(128)}) while((s32[]{:T(128)}, f32[16,2,512]{2,0,1:T(8,128)S(1)}, s32[]{:T(128)}, f32[512,2,512]{2,1,0:T(2,128)S(1)}, s32[]{:T(128)}) %tuple.40), condition=%wide.region_2.3_spmd, body=%wide.region_1.2_spmd.sunk | while | flops 201375744 | bytes 9306223 | solution.py:76
  533.6 1.6 fusion.122
  537.7 3.4 collective-permute-start
  541.1 4.9 collective-permute-done
  550.1 1.9 collective-permute-start
  552.1 6.3 collective-permute-done
  562.6 1.9 collective-permute-start
  564.5 6.3 collective-permute-done
  570.9 1.6 fusion.122
  575.0 1.9 collective-permute-start
  576.9 6.3 collective-permute-done
  587.4 1.9 collective-permute-start
  589.4 6.3 collective-permute-done
  599.9 1.9 collective-permute-start
  601.8 6.3 collective-permute-done
  608.2 1.6 fusion.122
  612.3 1.9 collective-permute-start
  614.2 6.3 collective-permute-done
  620.8 2.0 fusion.38
  622.8 1.9 fusion.45
  (100 shorter events, 43.0 us)
Async XLA Ops:
  6.5 4.6 copy-start.7
  6.5 346.8 %all-reduce.4.cloned.1.call-start = ((), (), s32[]{:S(2)}) async-start(), calls=%async_computation.2 | async-start | bytes 8388608
  8.4 26.3 %copy-start.6 = (bf16[2,512,1024]{2,1,0:T(8,128)(2,1)S(1)}, bf16[2,512,1024]{2,1,0:T(8,128)(2,1)}, u32[]{:S(2)}) copy-start(bf16[2,512,1024]{2,1,0:T(8,128)(2,1)} %param.5) | copy-start | bytes 6291460
  8.4 26.3 %collective-permute-start.2 = (bf16[1,512,1024]{2,1,0:T(8,128)(2,1)S(1)}, bf16[1,512,1024]{2,1,0:T(8,128)(2,1)S(1)}, u32[]{:S(2)}, u32[]{:S(2)}) collective-permute-start(bf16[1,512,1024]{2,1,0:T(8,128)(2,1)S(1)} %get-tuple-element.110), channel_id=1, source_target_pairs={{32,0},{64,32},{96,64},{128,96},{160,128},{192,160},{224,192},{0,2... | collective-permute-start | bytes 3145736 | tf_op jit(solution)/shard_map/ppermute | solution.py:10
  11.3 44.7 %collective-permute-start.1 = (bf16[1,512,1024]{2,1,0:T(8,128)(2,1)S(1)}, bf16[1,512,1024]{2,1,0:T(8,128)(2,1)S(1)}, u32[]{:S(2)}, u32[]{:S(2)}) collective-permute-start(bf16[1,512,1024]{2,1,0:T(8,128)(2,1)S(1)} %get-tuple-element.112), channel_id=1, source_target_pairs={{32,0},{64,32},{96,64},{128,96},{160,128},{192,160},{224,192},{0,2... | collective-permute-start | bytes 3145736 | tf_op jit(solution)/shard_map/ppermute | solution.py:10
  69.7 0.7 copy-start.8
  69.7 371.5 %all-gather.3.cloned.1.call-start = ((), (), s32[]{:S(2)}) async-start(), calls=%async_computation | async-start | bytes 4325376 | tf_op jit(solution)/shard_map/all_gather | solution.py:54
  354.9 175.4 %all-gather.5.cloned.1.call-start = ((), (), s32[]{:S(2)}) async-start(), calls=%async_computation.1 | async-start | bytes 2162688 | tf_op jit(solution)/shard_map/all_gather | solution.py:69
  448.4 2.2 copy-start.2
  448.4 2.2 copy-start.4
  448.4 3.4 copy-start
  537.7 8.3 %collective-permute-start = (f32[16,2,512]{2,0,1:T(8,128)S(1)}, f32[16,2,512]{2,0,1:T(8,128)S(1)}, u32[]{:S(2)}, u32[]{:S(2)}) collective-permute-start(f32[16,2,512]{2,0,1:T(8,128)S(1)} %pad_maximum_fusion.11), channel_id=1, source_target_pairs={{0,32},{32,64},{64,96},{96,128},{128,160},{160,192},{192,224},{1,3... | collective-permute-start | bytes 196616 | tf_op jit(solution)/shard_map/while/body/eval_jaxpr/ppermute | solution.py:16
  550.1 8.3 %collective-permute-start = (f32[16,2,512]{2,0,1:T(8,128)S(1)}, f32[16,2,512]{2,0,1:T(8,128)S(1)}, u32[]{:S(2)}, u32[]{:S(2)}) collective-permute-start(f32[16,2,512]{2,0,1:T(8,128)S(1)} %pad_maximum_fusion.11), channel_id=1, source_target_pairs={{0,32},{32,64},{64,96},{96,128},{128,160},{160,192},{192,224},{1,3... | collective-permute-start | bytes 196616 | tf_op jit(solution)/shard_map/while/body/eval_jaxpr/ppermute | solution.py:16
  562.6 8.3 %collective-permute-start = (f32[16,2,512]{2,0,1:T(8,128)S(1)}, f32[16,2,512]{2,0,1:T(8,128)S(1)}, u32[]{:S(2)}, u32[]{:S(2)}) collective-permute-start(f32[16,2,512]{2,0,1:T(8,128)S(1)} %pad_maximum_fusion.11), channel_id=1, source_target_pairs={{0,32},{32,64},{64,96},{96,128},{128,160},{160,192},{192,224},{1,3... | collective-permute-start | bytes 196616 | tf_op jit(solution)/shard_map/while/body/eval_jaxpr/ppermute | solution.py:16
  575.0 8.3 %collective-permute-start = (f32[16,2,512]{2,0,1:T(8,128)S(1)}, f32[16,2,512]{2,0,1:T(8,128)S(1)}, u32[]{:S(2)}, u32[]{:S(2)}) collective-permute-start(f32[16,2,512]{2,0,1:T(8,128)S(1)} %pad_maximum_fusion.11), channel_id=1, source_target_pairs={{0,32},{32,64},{64,96},{96,128},{128,160},{160,192},{192,224},{1,3... | collective-permute-start | bytes 196616 | tf_op jit(solution)/shard_map/while/body/eval_jaxpr/ppermute | solution.py:16
  587.4 8.3 %collective-permute-start = (f32[16,2,512]{2,0,1:T(8,128)S(1)}, f32[16,2,512]{2,0,1:T(8,128)S(1)}, u32[]{:S(2)}, u32[]{:S(2)}) collective-permute-start(f32[16,2,512]{2,0,1:T(8,128)S(1)} %pad_maximum_fusion.11), channel_id=1, source_target_pairs={{0,32},{32,64},{64,96},{96,128},{128,160},{160,192},{192,224},{1,3... | collective-permute-start | bytes 196616 | tf_op jit(solution)/shard_map/while/body/eval_jaxpr/ppermute | solution.py:16
  599.9 8.3 %collective-permute-start = (f32[16,2,512]{2,0,1:T(8,128)S(1)}, f32[16,2,512]{2,0,1:T(8,128)S(1)}, u32[]{:S(2)}, u32[]{:S(2)}) collective-permute-start(f32[16,2,512]{2,0,1:T(8,128)S(1)} %pad_maximum_fusion.11), channel_id=1, source_target_pairs={{0,32},{32,64},{64,96},{96,128},{128,160},{160,192},{192,224},{1,3... | collective-permute-start | bytes 196616 | tf_op jit(solution)/shard_map/while/body/eval_jaxpr/ppermute | solution.py:16
  612.3 8.3 %collective-permute-start = (f32[16,2,512]{2,0,1:T(8,128)S(1)}, f32[16,2,512]{2,0,1:T(8,128)S(1)}, u32[]{:S(2)}, u32[]{:S(2)}) collective-permute-start(f32[16,2,512]{2,0,1:T(8,128)S(1)} %pad_maximum_fusion.11), channel_id=1, source_target_pairs={{0,32},{32,64},{64,96},{96,128},{128,160},{160,192},{192,224},{1,3... | collective-permute-start | bytes 196616 | tf_op jit(solution)/shard_map/while/body/eval_jaxpr/ppermute | solution.py:16
  620.8 3.9 copy-start.5
  620.8 5.2 copy-start.1
  622.8 3.8 copy-start.3
Sparse Core Ops, SparseCore 0:
  69.8 283.4 all-reduce.3
  356.1 85.0 all-gather.2
  453.8 76.5 all-gather.4
where the time goes:
time: 636 us
  waiting for transfers between devices  530 us (83%)
  matrix products  34.8 us (5%)
  local copies, waits for them, and re-layouts  34.6 us (5%)
  starting transfers between devices  18.6 us (3%)
  between operations  13.9 us (2%)
    unnamed x4, waiting for transfers between devices  282 us
    all_gather x1, waiting for transfers between devices, shards(): margin_full = lax.all_gather(margin_rows, 'pw', axis=0, tiled=True)  86.2 us
    all_gather x1, waiting for transfers between devices, shards(): span_whole = lax.all_gather(own_span, 'pw', axis=0, tiled=True)  76.6 us
    ppermute x7, waiting for transfers between devices, shifted(): return lax.ppermute(shard, axis, pairs)  42.9 us
    ppermute x2, waiting for transfers between devices, from_behind(): return lax.ppermute(block, axis, route)  42.5 us
    ppermute x7, starting transfers between devices, shifted(): return lax.ppermute(shard, axis, pairs)  14.9 us
    slice x8, local copies, waits for them, and re-layouts, complex_rows(): right_re = right[:, 0]  14.8 us
  transfers between devices with their start and end apart: 12, of which 12 were waited for; matrix products, arithmetic and copies ran while one was open for 0% of the time, Pallas kernels for 0%

commit v1 on v0

--- a/solution.py
+++ b/solution.py
@@ -51,7 +51,9 @@
     margin_rows = lax.psum_scatter(
         jnp.stack([real_part, imag_part], 2), "pw", scatter_dimension=0, tiled=True
     )
-    margin_full = lax.all_gather(margin_rows, "pw", axis=0, tiled=True)
+    margin_full = jnp.concatenate(
+        lax.all_to_all(jnp.stack([margin_rows] * lax.axis_size("pw")), "pw", 0, 0), axis=0
+    )
     row_index = lax.broadcasted_iota(jnp.int32, (band_rows, bands), 0) + first_band
     col_index = lax.broadcasted_iota(jnp.int32, (band_rows, bands), 1)
     eye_real = (row_index == col_index).astype(jnp.float32)

time: 636 us -> 659 us (1.036)
  waiting for transfers between devices: 530 us -> 542 us
  starting transfers between devices: 18.6 us -> 25.7 us
    all_to_all x0 -> x1, waiting for transfers between devices: none -> 96.6 us  [shards(): lax.all_to_all(jnp.stack([margin_rows] * lax.axis_size('pw')), 'pw', 0, 0)]
    all_gather x1 -> x0, waiting for transfers between devices: 86.2 us -> none  [shards(): margin_full = lax.all_gather(margin_rows, 'pw', axis=0, tiled=True)]
    all_to_all x0 -> x1, starting transfers between devices: none -> 7.16 us  [shards(): lax.all_to_all(jnp.stack([margin_rows] * lax.axis_size('pw')), 'pw', 0, 0)]
    unnamed x4 -> x3, waiting for transfers between devices: 282 us -> 282 us
where the time goes in v1:
time: 659 us; the launch traced here: 658 us
  waiting for transfers between devices  542 us (82%)
  local copies, waits for them, and re-layouts  37.9 us (6%)
  matrix products  34.8 us (5%)
  starting transfers between devices  25.7 us (4%)
  between operations  14.2 us (2%)
    unnamed x3, waiting for transfers between devices  282 us
    all_to_all x1, waiting for transfers between devices, shards(): lax.all_to_all(jnp.stack([margin_rows] * lax.axis_size('pw')), 'pw', 0, 0)  96.6 us
    all_gather x1, waiting for transfers between devices, shards(): span_whole = lax.all_gather(own_span, 'pw', axis=0, tiled=True)  77.8 us
    ppermute x7, waiting for transfers between devices, shifted(): return lax.ppermute(shard, axis, pairs)  42.9 us
    ppermute x2, waiting for transfers between devices, from_behind(): return lax.ppermute(block, axis, route)  42.5 us
    ppermute x7, starting transfers between devices, shifted(): return lax.ppermute(shard, axis, pairs)  14.9 us
    slice x8, local copies, waits for them, and re-layouts, complex_rows(): right_re = right[:, 0]  14.8 us
  transfers between devices with their start and end apart: 12, of which 12 were waited for; matrix products, arithmetic and copies ran while one was open for 0% of the time, Pallas kernels for 0%

profile of v1, /device:TPU:8, one launch (start us, length us, event | category | flops | bytes accessed | tf_op | source)
XLA Modules:
  0.0 658.2 jit_solution(8680311088206526470)
XLA Ops:
  6.5 1.9 fusion.87
  8.4 2.7 collective-permute-start.2
  12.2 22.5 %collective-permute-done.2 = bf16[1,512,1024]{2,1,0:T(8,128)(2,1)S(1)} collective-permute-done((bf16[1,512,1024]{2,1,0:T(8,128)(2,1)S(1)}, bf16[1,512,1024]{2,1,0:T(8,128)(2,1)S(1)}, u32[]{:S(2)}, u32[]{:S(2)}) %collective-permute-start.2) | collective-permute-done | bytes 1048608 | tf_op jit(solution)/shard_map/ppermute | solution.py:10
  36.0 20.1 %collective-permute-done.1 = bf16[1,512,1024]{2,1,0:T(8,128)(2,1)S(1)} collective-permute-done((bf16[1,512,1024]{2,1,0:T(8,128)(2,1)S(1)}, bf16[1,512,1024]{2,1,0:T(8,128)(2,1)S(1)}, u32[]{:S(2)}, u32[]{:S(2)}) %collective-permute-start.1) | collective-permute-done | bytes 1048608 | tf_op jit(solution)/shard_map/ppermute | solution.py:10
  59.9 2.4 pad_maximum_fusion.1
  62.3 7.3 %copy.6 = f32[512,2,2,512]{3,2,1,0:T(2,128)} copy(f32[512,2,2,512]{0,3,1,2:T(8,128)} %pad_maximum_fusion.1) | data formatting | bytes 8388608 | tf_op jit(solution)/shard_map/stack | solution.py:52
  71.6 281.8 %all-reduce.4.cloned.1.call-done = f32[512,2,2,512]{3,2,1,0:T(2,128)} async-done(((f32[512,2,2,512]{3,2,1,0:T(2,128)}), f32[512,2,2,512]{3,2,1,0:T(2,128)}) %all-reduce.4.cloned.1.call-update) | async-done | bytes 4194320
  354.3 3.9 stack.112
  358.2 7.2 %all-to-all-start = ((f32[32,16,2,2,512]{4,3,2,1,0:T(2,128)}), f32[32,16,2,2,512]{4,3,2,1,0:T(2,128)}, u32[]{:S(2)}, u32[]{:S(2)}) async-start(f32[32,16,2,2,512]{4,3,2,1,0:T(2,128)} %stack.112), calls=%async_computation | async-start | bytes 8388608 | tf_op jit(solution)/shard_map/all_to_all | solution.py:55
  365.4 96.6 %all-to-all-done = f32[32,16,2,2,512]{4,3,2,1,0:T(2,128)} async-done(((f32[32,16,2,2,512]{4,3,2,1,0:T(2,128)}), f32[32,16,2,2,512]{4,3,2,1,0:T(2,128)}, u32[]{:S(2)}, u32[]{:S(2)}) %all-to-all-start) | async-done | bytes 4194336 | tf_op jit(solution)/shard_map/all_to_all | solution.py:55
  462.0 3.7 slice_bitcast_fusion
  465.7 3.5 fusion.85
  474.6 77.8 %all-gather.2.cloned.1.call-done = f32[512,2,512]{2,0,1:T(8,128)} async-done(((f32[16,2,512]{2,0,1:T(8,128)}), f32[512,2,512]{2,0,1:T(8,128)}) %all-gather.2.cloned.1.call-update) | async-done | bytes 2097168 | tf_op jit(solution)/shard_map/all_gather | solution.py:71
  552.4 3.2 copy.7
  555.6 87.2 %while.13 = (s32[]{:T(128)}, f32[16,2,512]{2,0,1:T(8,128)S(1)}, s32[]{:T(128)}, f32[512,2,512]{2,1,0:T(2,128)S(1)}, s32[]{:T(128)}) while((s32[]{:T(128)}, f32[16,2,512]{2,0,1:T(8,128)S(1)}, s32[]{:T(128)}, f32[512,2,512]{2,1,0:T(2,128)S(1)}, s32[]{:T(128)}) %tuple.40), condition=%wide.region_2.3_spmd, body=%wide.region_1.2_spmd.sunk | while | flops 201375744 | bytes 9306223 | solution.py:78
  559.7 3.4 collective-permute-start
  563.1 4.9 collective-permute-done
  572.2 1.9 collective-permute-start
  574.1 6.3 collective-permute-done
  580.5 1.6 fusion.122
  584.6 1.9 collective-permute-start
  586.5 6.3 collective-permute-done
  597.0 1.9 collective-permute-start
  599.0 6.3 collective-permute-done
  609.5 1.9 collective-permute-start
  611.4 6.3 collective-permute-done
  621.9 1.9 collective-permute-start
  623.8 6.3 collective-permute-done
  634.3 1.9 collective-permute-start
  636.3 6.3 collective-permute-done
  642.9 2.0 fusion.38
  644.8 1.9 fusion.45
  (100 shorter events, 45.6 us)
Async XLA Ops:
  6.5 4.6 copy-start.7
  6.5 346.8 %all-reduce.4.cloned.1.call-start = ((), (), s32[]{:S(2)}) async-start(), calls=%async_computation.2 | async-start | bytes 8388608
  8.4 26.3 %copy-start.6 = (bf16[2,512,1024]{2,1,0:T(8,128)(2,1)S(1)}, bf16[2,512,1024]{2,1,0:T(8,128)(2,1)}, u32[]{:S(2)}) copy-start(bf16[2,512,1024]{2,1,0:T(8,128)(2,1)} %param.5) | copy-start | bytes 6291460
  8.4 26.3 %collective-permute-start.2 = (bf16[1,512,1024]{2,1,0:T(8,128)(2,1)S(1)}, bf16[1,512,1024]{2,1,0:T(8,128)(2,1)S(1)}, u32[]{:S(2)}, u32[]{:S(2)}) collective-permute-start(bf16[1,512,1024]{2,1,0:T(8,128)(2,1)S(1)} %get-tuple-element.110), channel_id=1, source_target_pairs={{32,0},{64,32},{96,64},{128,96},{160,128},{192,160},{224,192},{0,2... | collective-permute-start | bytes 3145736 | tf_op jit(solution)/shard_map/ppermute | solution.py:10
  11.3 44.7 %collective-permute-start.1 = (bf16[1,512,1024]{2,1,0:T(8,128)(2,1)S(1)}, bf16[1,512,1024]{2,1,0:T(8,128)(2,1)S(1)}, u32[]{:S(2)}, u32[]{:S(2)}) collective-permute-start(bf16[1,512,1024]{2,1,0:T(8,128)(2,1)S(1)} %get-tuple-element.112), channel_id=1, source_target_pairs={{32,0},{64,32},{96,64},{128,96},{160,128},{192,160},{224,192},{0,2... | collective-permute-start | bytes 3145736 | tf_op jit(solution)/shard_map/ppermute | solution.py:10
  69.7 0.7 copy-start.8
  358.2 103.8 %all-to-all-start = ((f32[32,16,2,2,512]{4,3,2,1,0:T(2,128)}), f32[32,16,2,2,512]{4,3,2,1,0:T(2,128)}, u32[]{:S(2)}, u32[]{:S(2)}) async-start(f32[32,16,2,2,512]{4,3,2,1,0:T(2,128)} %stack.112), calls=%async_computation | async-start | bytes 8388608 | tf_op jit(solution)/shard_map/all_to_all | solution.py:55
  365.3 187.1 %all-gather.2.cloned.1.call-start = ((), (), s32[]{:S(2)}) async-start(), calls=%async_computation.1 | async-start | bytes 2162688 | tf_op jit(solution)/shard_map/all_gather | solution.py:71
  469.1 2.2 copy-start.2
  469.1 2.2 copy-start.4
  469.2 3.4 copy-start
  559.7 8.3 %collective-permute-start = (f32[16,2,512]{2,0,1:T(8,128)S(1)}, f32[16,2,512]{2,0,1:T(8,128)S(1)}, u32[]{:S(2)}, u32[]{:S(2)}) collective-permute-start(f32[16,2,512]{2,0,1:T(8,128)S(1)} %pad_maximum_fusion.11), channel_id=1, source_target_pairs={{0,32},{32,64},{64,96},{96,128},{128,160},{160,192},{192,224},{1,3... | collective-permute-start | bytes 196616 | tf_op jit(solution)/shard_map/while/body/eval_jaxpr/ppermute | solution.py:16
  572.2 8.3 %collective-permute-start = (f32[16,2,512]{2,0,1:T(8,128)S(1)}, f32[16,2,512]{2,0,1:T(8,128)S(1)}, u32[]{:S(2)}, u32[]{:S(2)}) collective-permute-start(f32[16,2,512]{2,0,1:T(8,128)S(1)} %pad_maximum_fusion.11), channel_id=1, source_target_pairs={{0,32},{32,64},{64,96},{96,128},{128,160},{160,192},{192,224},{1,3... | collective-permute-start | bytes 196616 | tf_op jit(solution)/shard_map/while/body/eval_jaxpr/ppermute | solution.py:16
  584.6 8.3 %collective-permute-start = (f32[16,2,512]{2,0,1:T(8,128)S(1)}, f32[16,2,512]{2,0,1:T(8,128)S(1)}, u32[]{:S(2)}, u32[]{:S(2)}) collective-permute-start(f32[16,2,512]{2,0,1:T(8,128)S(1)} %pad_maximum_fusion.11), channel_id=1, source_target_pairs={{0,32},{32,64},{64,96},{96,128},{128,160},{160,192},{192,224},{1,3... | collective-permute-start | bytes 196616 | tf_op jit(solution)/shard_map/while/body/eval_jaxpr/ppermute | solution.py:16
  597.0 8.3 %collective-permute-start = (f32[16,2,512]{2,0,1:T(8,128)S(1)}, f32[16,2,512]{2,0,1:T(8,128)S(1)}, u32[]{:S(2)}, u32[]{:S(2)}) collective-permute-start(f32[16,2,512]{2,0,1:T(8,128)S(1)} %pad_maximum_fusion.11), channel_id=1, source_target_pairs={{0,32},{32,64},{64,96},{96,128},{128,160},{160,192},{192,224},{1,3... | collective-permute-start | bytes 196616 | tf_op jit(solution)/shard_map/while/body/eval_jaxpr/ppermute | solution.py:16
  609.5 8.3 %collective-permute-start = (f32[16,2,512]{2,0,1:T(8,128)S(1)}, f32[16,2,512]{2,0,1:T(8,128)S(1)}, u32[]{:S(2)}, u32[]{:S(2)}) collective-permute-start(f32[16,2,512]{2,0,1:T(8,128)S(1)} %pad_maximum_fusion.11), channel_id=1, source_target_pairs={{0,32},{32,64},{64,96},{96,128},{128,160},{160,192},{192,224},{1,3... | collective-permute-start | bytes 196616 | tf_op jit(solution)/shard_map/while/body/eval_jaxpr/ppermute | solution.py:16
  621.9 8.3 %collective-permute-start = (f32[16,2,512]{2,0,1:T(8,128)S(1)}, f32[16,2,512]{2,0,1:T(8,128)S(1)}, u32[]{:S(2)}, u32[]{:S(2)}) collective-permute-start(f32[16,2,512]{2,0,1:T(8,128)S(1)} %pad_maximum_fusion.11), channel_id=1, source_target_pairs={{0,32},{32,64},{64,96},{96,128},{128,160},{160,192},{192,224},{1,3... | collective-permute-start | bytes 196616 | tf_op jit(solution)/shard_map/while/body/eval_jaxpr/ppermute | solution.py:16
  634.3 8.3 %collective-permute-start = (f32[16,2,512]{2,0,1:T(8,128)S(1)}, f32[16,2,512]{2,0,1:T(8,128)S(1)}, u32[]{:S(2)}, u32[]{:S(2)}) collective-permute-start(f32[16,2,512]{2,0,1:T(8,128)S(1)} %pad_maximum_fusion.11), channel_id=1, source_target_pairs={{0,32},{32,64},{64,96},{96,128},{128,160},{160,192},{192,224},{1,3... | collective-permute-start | bytes 196616 | tf_op jit(solution)/shard_map/while/body/eval_jaxpr/ppermute | solution.py:16
  642.8 3.9 copy-start.5
  642.8 5.2 copy-start.1
  644.8 3.8 copy-start.3
Sparse Core Ops, SparseCore 0:
  69.8 283.4 all-reduce.3
  474.6 77.7 all-gather.1
